TPU v7x, 32 devices: a whole 2x2x4 slice. The times are simulated.
32 devices in a mesh: seg: 4 (over z), blk: 8 (over y, x, core).
Axes of the slice: x: 2, y: 2, z: 4, core: 2. Of those that a mesh axis runs over, the one named last changes fastest.
Arguments:
- train_acts: bfloat16 [4, 1024, 512], P('seg', 'blk'), may hold values from -6 to 6
- train_grads: bfloat16 [4, 1024, 4096], P('seg', 'blk'), may hold values from -0.0059814453 to 0.0059814453
- counts: int32 [8], replicated, may hold values from 1 to 2, as said below
- basis_in: bfloat16 [4, 1, 512, 512], P('seg'), may hold values from -1 to 1, as said below
- basis_out: bfloat16 [4, 8, 512, 512], P('seg', 'blk'), may hold values from -1 to 1, as said below
- eigenvalues: bfloat16 [4, 8, 512, 512], P('seg', 'blk'), may hold values from 0.049804688 to 5
- back_weight: bfloat16 [4, 8, 512, 512], P('seg', 'blk'), may hold values from -0.25 to 0.25
- derivative: bfloat16 [4, 4, 32, 4096], P('seg', None, None, 'blk'), may hold values from 0 to 1
- query_acts: bfloat16 [4, 4, 32, 512], P('seg'), may hold values from -6 to 6
- query_top: bfloat16 [4, 32, 4096], P(None, None, 'blk'), may hold values from -0.0059814453 to 0.0059814453
Outputs:
- scores: float32 [4, 16], P(None, 'blk')
Inputs may be any that keep to these rules, and one draw needn't show every extreme that they name: In each pair of indices 2k and 2k+1 of blk one count is 2 and the other 1, so all counts add up to 12; slots below a device's count are valid. `basis_in`: each 512 x 512 matrix is orthogonal up to rounding. `basis_out`: each 512 x 512 matrix is orthogonal up to rounding.
All inputs are finite; a program needn't handle non-finite values.
Results may differ from a plain program's by a relative error of at most 0.015.
Values may be sent and summed in bfloat16 or wider, within the bound.
A program may use at most 64 MiB of HBM per device.

v0:
```python
import math

import jax
import jax.numpy as jnp
from jax import lax
from jax.sharding import PartitionSpec as P

TB = 64
SLOTS = 2


damping = 0.05


def passed_along(value, axis, steps):
    count = lax.axis_size(axis)
    first, last = (max(0, -steps), min(count, count - steps))
    return lax.ppermute(value, axis, [(source, source + steps) for source in range(first, last)])


def advance(current, weight, derivs):
    queries, query_tok, blk_width = current.shape
    mixed = jnp.dot(
        current.reshape(queries * query_tok, blk_width), weight, preferred_element_type=jnp.float32
    )
    mixed = mixed.reshape(queries, query_tok, blk_width)
    return (current.astype(jnp.float32) + mixed * derivs.astype(jnp.float32)).astype(jnp.bfloat16)


def precondition(current, acts_seg, inner_basis, outer_basis, eigen_block):
    queries, query_tok, blk_width = current.shape
    in_slices = inner_basis.shape[0]
    in_width = in_slices * blk_width
    rot_err = jnp.dot(
        current.reshape(queries * query_tok, blk_width),
        outer_basis,
        preferred_element_type=jnp.float32,
    )
    rot_err = rot_err.astype(jnp.bfloat16).reshape(queries, query_tok, blk_width)
    act_split = acts_seg.reshape(queries, query_tok, in_slices, blk_width)
    rot_acts = jnp.einsum(
        "qtid,ide->qtie", act_split, inner_basis, preferred_element_type=jnp.float32
    ).astype(jnp.bfloat16)
    core_raw = jnp.einsum("qtd,qtie->qdie", rot_err, rot_acts, preferred_element_type=jnp.float32)
    core_raw = core_raw.reshape(queries, blk_width, in_width)
    scaled_core = (core_raw / (eigen_block.astype(jnp.float32)[None] + damping)).astype(
        jnp.bfloat16
    )
    left_prod = jnp.einsum(
        "cd,qdf->qcf", outer_basis, scaled_core, preferred_element_type=jnp.float32
    ).astype(jnp.bfloat16)
    left_split = left_prod.reshape(queries, blk_width, in_slices, blk_width)
    precond = jnp.einsum(
        "qcie,ife->qcif", left_split, inner_basis, preferred_element_type=jnp.float32
    )
    return precond.astype(jnp.bfloat16).reshape(queries, blk_width, in_width)


def block_scores(grad_rows, act_rows, precond, slot_tokens):
    row_count = grad_rows.shape[0]
    group_count = max(row_count // slot_tokens, 1)
    group_rows = row_count // group_count
    batch_groups = math.gcd(group_count, 8)
    grad_groups = grad_rows.reshape(
        group_count // batch_groups, batch_groups, group_rows, grad_rows.shape[1]
    )
    act_groups = act_rows.reshape(
        group_count // batch_groups, batch_groups, group_rows, act_rows.shape[1]
    )

    def one_batch(operands):
        grad_block, act_block = operands
        outer_prod = jnp.einsum(
            "btd,bte->bde", grad_block, act_block, preferred_element_type=jnp.float32
        ).astype(jnp.bfloat16)
        return jnp.einsum("bde,qde->bq", outer_prod, precond, preferred_element_type=jnp.float32)

    partial_scores = lax.map(one_batch, (grad_groups, act_groups))
    return (partial_scores.reshape(group_count, precond.shape[0]), group_rows)


def body(
    train_acts,
    train_grads,
    counts,
    basis_in,
    basis_out,
    eigenvalues,
    back_weight,
    derivative,
    query_acts,
    query_top,
):
    seg_count = lax.axis_size("seg")
    seg_index = lax.axis_index("seg")
    blk_index = lax.axis_index("blk")
    n_slot = lax.axis_size("blk") * SLOTS
    slot_ids = jnp.arange(n_slot, dtype=jnp.int32)
    current = query_top
    for relay_step in range(seg_count - 1):
        moved = advance(current, back_weight[0, 0], derivative[0])
        arrived = passed_along(moved, "seg", -1)
        current = jnp.where(seg_index == seg_count - 2 - relay_step, arrived, current)
    precond = precondition(current, query_acts[0], basis_in[0], basis_out[0, 0], eigenvalues[0, 0])
    exchanged = lax.all_to_all(train_grads, "blk", split_axis=2, concat_axis=1, tiled=True)
    grad_rows = exchanged[0]
    scores_part, group_rows = block_scores(
        grad_rows, lax.all_gather(train_acts, "blk", axis=1, tiled=True)[0], precond, TB
    )
    slot_of = jnp.arange(scores_part.shape[0], dtype=jnp.int32) * group_rows // TB
    placement = (slot_of[:, None] == slot_ids[None, :]).astype(jnp.float32)
    local_scores = jnp.dot(scores_part.T, placement, precision=lax.Precision.HIGHEST)
    mine = lax.psum_scatter(local_scores, "blk", scatter_dimension=1, tiled=True)
    mine = lax.psum(mine, "seg")
    own_valid = (jnp.arange(SLOTS, dtype=jnp.int32) < counts[blk_index]).astype(jnp.float32)
    return mine * own_valid[None, :]


def solution(mesh):
    in_specs = (
        P("seg", "blk", None),
        P("seg", "blk", None),
        P(),
        P("seg", None, None, None),
        P("seg", "blk", None, None),
        P("seg", "blk", None, None),
        P("seg", "blk", None, None),
        P("seg", None, None, "blk"),
        P("seg", None, None, None),
        P(None, None, "blk"),
    )
    out_specs = P(None, "blk")
    return jax.shard_map(body, mesh=mesh, in_specs=in_specs, out_specs=out_specs, check_vma=False)
```

profile of v0, /device:TPU:0, one launch (start us, length us, event | category | flops | bytes accessed | tf_op | source)
XLA Modules:
  0.0 125.0 jit_solution(6837176893961638313)
XLA Ops:
  6.5 1.4 %fusion.15 = bf16[4,32,512]{2,1,0:T(8,128)(2,1)S(1)} fusion(bf16[4,32,512]{2,1,0:T(8,128)(2,1)} %param.21, bf16[1,1,512,512]{3,2,1,0:T(8,128)(2,1)} %param.18, bf16[1,4,32,512]{3,2,1,0:T(8,128)(2,1)} %param.19), kind=kOutput, calls=%fused_computation.20 | convolution fusion | flops 67436544 | bytes 917504 | tf_op jit(solution)/shard_map/dot_general | solution.py:23
  8.0 1.3 %collective-permute-start = (bf16[4,32,512]{2,1,0:T(8,128)(2,1)S(1)}, bf16[4,32,512]{2,1,0:T(8,128)(2,1)S(1)}, u32[]{:S(2)}, u32[]{:S(2)}) collective-permute-start(bf16[4,32,512]{2,1,0:T(8,128)(2,1)S(1)} %fusion.15), channel_id=1, source_target_pairs={{8,0},{16,8},{24,16},{9,1},{17,9},{25,17},{10,2},{18,10},{26,18},{... | collective-permute-start | bytes 393224 | tf_op jit(solution)/shard_map/ppermute | solution.py:18
  9.3 5.0 %copy.25 = bf16[1,128,4096]{1,0,2:T(2,128)(2,1)S(1)} copy(bf16[1,128,4096]{2,1,0:T(8,128)(2,1)} %param.13) | data formatting | bytes 2097152 | tf_op args[1]
  14.8 23.4 %reduce = bf16[4096,128]{1,0:T(8,128)(2,1)} reduce(bf16[4096,1,128]{2,1,0:T(2,128)(2,1)S(1)} %bitcast.92, bf16[]{:T(256)} %broadcast.63), dimensions={1}, to_apply=%bitcast.73.reduce_sub_computation | reduce | bytes 2097154
  38.2 2.2 %reshape.95 = bf16[8,2,32768]{2,1,0:T(2,128)(2,1)} reshape(bf16[4096,128]{1,0:T(8,128)(2,1)} %reduce) | data formatting | bytes 2097152
  40.4 5.3 %all-to-all-start = ((bf16[8,2,32768]{2,1,0:T(2,128)(2,1)}), bf16[8,2,32768]{2,1,0:T(2,128)(2,1)}, u32[]{:S(2)}, u32[]{:S(2)}) async-start(bf16[8,2,32768]{2,1,0:T(2,128)(2,1)} %reshape.95), calls=%async_computation | async-start | bytes 2097152 | tf_op jit(solution)/shard_map/all_to_all | solution.py:105
  46.9 1.3 %collective-permute-start.1 = (bf16[4,32,512]{2,1,0:T(8,128)(2,1)S(1)}, bf16[4,32,512]{2,1,0:T(8,128)(2,1)S(1)}, u32[]{:S(2)}, u32[]{:S(2)}) collective-permute-start(bf16[4,32,512]{2,1,0:T(8,128)(2,1)S(1)} %add_convert_fusion.1), channel_id=1, source_target_pairs={{8,0},{16,8},{24,16},{9,1},{17,9},{25,17},{10,2},{18,10},{26,18},{... | collective-permute-start | bytes 393224 | tf_op jit(solution)/shard_map/ppermute | solution.py:18
  48.3 7.2 %collective-permute-done.1 = bf16[4,32,512]{2,1,0:T(8,128)(2,1)S(1)} collective-permute-done((bf16[4,32,512]{2,1,0:T(8,128)(2,1)S(1)}, bf16[4,32,512]{2,1,0:T(8,128)(2,1)S(1)}, u32[]{:S(2)}, u32[]{:S(2)}) %collective-permute-start.1) | collective-permute-done | bytes 131104 | tf_op jit(solution)/shard_map/ppermute | solution.py:18
  55.8 1.5 %collective-permute-start.2 = (bf16[4,32,512]{2,1,0:T(8,128)(2,1)S(1)}, bf16[4,32,512]{2,1,0:T(8,128)(2,1)S(1)}, u32[]{:S(2)}, u32[]{:S(2)}) collective-permute-start(bf16[4,32,512]{2,1,0:T(8,128)(2,1)S(1)} %add_convert_fusion), channel_id=1, source_target_pairs={{8,0},{16,8},{24,16},{9,1},{17,9},{25,17},{10,2},{18,10},{26,18},{... | collective-permute-start | bytes 393224 | tf_op jit(solution)/shard_map/ppermute | solution.py:18
  57.3 1.3 %fusion.16 = bf16[4,32,512]{2,1,0:T(8,128)(2,1)S(1)} fusion(bf16[1,1,512,512]{3,2,1,0:T(8,128)(2,1)} %param.15, bf16[1,4,32,512]{3,2,1,0:T(8,128)(2,1)S(1)} %copy-done.7), kind=kOutput, calls=%fused_computation.21 | convolution fusion | flops 67174400 | bytes 786432 | tf_op jit(solution)/shard_map/qtid,ide->qtie/dot_general | solution.py:41
  60.5 2.7 %collective-permute-done.2 = bf16[4,32,512]{2,1,0:T(8,128)(2,1)S(1)} collective-permute-done((bf16[4,32,512]{2,1,0:T(8,128)(2,1)S(1)}, bf16[4,32,512]{2,1,0:T(8,128)(2,1)S(1)}, u32[]{:S(2)}, u32[]{:S(2)}) %collective-permute-start.2) | collective-permute-done | bytes 131104 | tf_op jit(solution)/shard_map/ppermute | solution.py:18
  63.5 3.2 %fusion.13 = bf16[4,512,512]{2,1,0:T(8,128)(2,1)} fusion(bf16[4,32,512]{2,1,0:T(8,128)(2,1)S(1)} %bitcast.96, bf16[4,32,512]{2,1,0:T(8,128)(2,1)S(1)} %fusion.16, f32[512,512]{1,0:T(8,128)S(1)} %add_bitcast_fusion, bf16[1,1,512,512]{3,2,1,0:T(8,128)(2,1)S(1)} %copy-done), kind=kOutput, calls=%fused_computation.13 | convolution fusion | flops 1142947840 | bytes 3932160 | tf_op jit(solution)/shard_map/cd,qdf->qcf/dot_general | solution.py:49
  66.7 2.9 %fusion.10 = bf16[4,512,512]{2,1,0:T(8,128)(2,1)S(1)} fusion(bf16[4,512,512]{2,1,0:T(8,128)(2,1)} %fusion.13, bf16[1,1,512,512]{3,2,1,0:T(8,128)(2,1)S(1)} %copy-done.6), kind=kOutput, calls=%fused_computation.12 | convolution fusion | flops 1074790400 | bytes 4718592 | tf_op jit(solution)/shard_map/qcie,ife->qcif/dot_general | solution.py:53
  69.6 3.0 %copy.29 = bf16[4,512,512]{2,0,1:T(4,128)(2,1)} copy(bf16[4,512,512]{2,1,0:T(8,128)(2,1)S(1)} %fusion.10) | data formatting | bytes 4194304 | tf_op jit(solution)/shard_map/while | solution.py:78
  72.5 4.3 %reshape.96 = bf16[4096,1,128]{2,1,0:T(2,128)(2,1)S(1)} reshape(bf16[8,2,32768]{2,1,0:T(2,128)(2,1)} %all-to-all-done) | data formatting | bytes 2097152
  76.9 1.1 copy.35
  78.0 1.5 %copy.26 = bf16[1,8,128,512]{3,2,1,0:T(8,128)(2,1)S(1)} copy(bf16[1,8,128,512]{2,3,1,0:T(8,128)(2,1)} %bitcast.94) | data formatting | bytes 2097152 | tf_op jit(solution)/shard_map/all_to_all | solution.py:105
  79.5 12.8 %while.10 = (s32[]{:T(128)}, f32[2,8,4]{1,0,2:T(2,128)S(1)}, bf16[2,8,64,512]{3,2,1,0:T(8,128)(2,1)S(1)}, bf16[2,8,64,512]{3,2,1,0:T(8,128)(2,1)}, bf16[4,512,512]{2,0,1:T(4,128)(2,1)}, /*index=5*/s32[]{:T(128)}, s32[]{:T(128)}) while((s32[]{:T(128)}, f32[2,8,4]{1,0,2:T(2,128)S(1)}, bf16[2,8,64,512]{3,2,1,0:T(8,128)(2,1)S(1)}, ...), condition=%wide.region_1.2_spmd, body=%wide.region_0.1_spmd.sunk | while | flops 287309824 | bytes 19924460 | solution.py:78
  79.5 2.5 %convolution_convert_fusion.4 = bf16[8,512,512]{2,1,0:T(8,128)(2,1)S(1)} fusion(bf16[2,8,64,512]{3,2,1,0:T(8,128)(2,1)} %get-tuple-element.111, s32[]{:T(128)} %get-tuple-element.101, bf16[2,8,64,512]{3,2,1,0:T(8,128)(2,1)S(1)} %get-tuple-element.110), kind=kOutput, calls=%fused_computation.2.clone.1 | convolution fusion | flops 270532608 | bytes 5243904 | tf_op jit(solution)/shard_map/while/body/eval_jaxpr/btd,bte->bde/dot_general | solution.py:73
  82.0 3.8 %fusion.47 = f32[8,4,1]{0,1,2:T(4,128)S(1)} fusion(bf16[4,512,512]{2,0,1:T(4,128)(2,1)S(1)} %copy-done.2, bf16[8,512,512]{2,1,0:T(8,128)(2,1)S(1)} %convolution_convert_fusion.4), kind=kOutput, calls=%fused_computation.clone.1 | convolution fusion | flops 16777216 | bytes 6291584 | tf_op jit(solution)/shard_map/while/body/eval_jaxpr/bde,qde->bq/dot_general | solution.py:76
  85.9 2.5 %convolution_convert_fusion.4 = bf16[8,512,512]{2,1,0:T(8,128)(2,1)S(1)} fusion(bf16[2,8,64,512]{3,2,1,0:T(8,128)(2,1)} %get-tuple-element.111, s32[]{:T(128)} %get-tuple-element.101, bf16[2,8,64,512]{3,2,1,0:T(8,128)(2,1)S(1)} %get-tuple-element.110), kind=kOutput, calls=%fused_computation.2.clone.1 | convolution fusion | flops 270532608 | bytes 5243904 | tf_op jit(solution)/shard_map/while/body/eval_jaxpr/btd,bte->bde/dot_general | solution.py:73
  88.4 3.8 %fusion.47 = f32[8,4,1]{0,1,2:T(4,128)S(1)} fusion(bf16[4,512,512]{2,0,1:T(4,128)(2,1)S(1)} %copy-done.2, bf16[8,512,512]{2,1,0:T(8,128)(2,1)S(1)} %convolution_convert_fusion.4), kind=kOutput, calls=%fused_computation.clone.1 | convolution fusion | flops 16777216 | bytes 6291584 | tf_op jit(solution)/shard_map/while/body/eval_jaxpr/bde,qde->bq/dot_general | solution.py:76
  92.6 13.1 %all-reduce = f32[4,16]{0,1:T(8,128)S(1)} all-reduce(f32[4,16]{0,1:T(8,128)S(1)} %fusion.29), channel_id=2, replica_groups=mesh['seg'=4,'blk'=8] {'blk'}, use_global_device_ids=true, to_apply=%region_2.3.clone | all-reduce | flops 64 | bytes 512
  106.4 11.2 %psum.7 = f32[4,2]{0,1:T(2,128)S(1)} all-reduce(f32[4,2]{0,1:T(2,128)S(1)} %constant_dynamic-slice_fusion), channel_id=1, replica_groups=mesh['seg'=4,'blk'=8] {'seg'}, use_global_device_ids=true, to_apply=%region_3.4 | all-reduce | flops 8 | bytes 64 | tf_op jit(solution)/shard_map/psum | solution.py:114
  (45 shorter events, 5.2 us)
Async XLA Ops:
  6.5 56.7 %copy-start = (bf16[1,1,512,512]{3,2,1,0:T(8,128)(2,1)S(1)}, bf16[1,1,512,512]{3,2,1,0:T(8,128)(2,1)}, u32[]{:S(2)}) copy-start(bf16[1,1,512,512]{3,2,1,0:T(8,128)(2,1)} %param.16) | copy-start | bytes 1572868
  8.0 38.5 %collective-permute-start = (bf16[4,32,512]{2,1,0:T(8,128)(2,1)S(1)}, bf16[4,32,512]{2,1,0:T(8,128)(2,1)S(1)}, u32[]{:S(2)}, u32[]{:S(2)}) collective-permute-start(bf16[4,32,512]{2,1,0:T(8,128)(2,1)S(1)} %fusion.15), channel_id=1, source_target_pairs={{8,0},{16,8},{24,16},{9,1},{17,9},{25,17},{10,2},{18,10},{26,18},{... | collective-permute-start | bytes 393224 | tf_op jit(solution)/shard_map/ppermute | solution.py:18
  38.2 8.3 %copy-start.5 = (bf16[4,32,512]{2,1,0:T(8,128)(2,1)S(1)}, bf16[4,32,512]{2,1,0:T(8,128)(2,1)}, u32[]{:S(2)}) copy-start(bf16[4,32,512]{2,1,0:T(8,128)(2,1)} %param.21) | copy-start | bytes 393220
  38.2 8.4 %copy-start.1 = (bf16[1,1,512,512]{3,2,1,0:T(8,128)(2,1)S(1)}, bf16[1,1,512,512]{3,2,1,0:T(8,128)(2,1)}, u32[]{:S(2)}) copy-start(bf16[1,1,512,512]{3,2,1,0:T(8,128)(2,1)} %param.18) | copy-start | bytes 1572868
  38.2 8.4 %copy-start.4 = (bf16[1,4,32,512]{3,2,1,0:T(8,128)(2,1)S(1)}, bf16[1,4,32,512]{3,2,1,0:T(8,128)(2,1)}, u32[]{:S(2)}) copy-start(bf16[1,4,32,512]{3,2,1,0:T(8,128)(2,1)} %param.19) | copy-start | bytes 393220
  40.4 7.7 %copy-start.3 = (bf16[1,1,512,512]{3,2,1,0:T(8,128)(2,1)S(1)}, bf16[1,1,512,512]{3,2,1,0:T(8,128)(2,1)}, u32[]{:S(2)}) copy-start(bf16[1,1,512,512]{3,2,1,0:T(8,128)(2,1)} %param.17) | copy-start | bytes 1572868
  40.4 32.1 %all-to-all-start = ((bf16[8,2,32768]{2,1,0:T(2,128)(2,1)}), bf16[8,2,32768]{2,1,0:T(2,128)(2,1)}, u32[]{:S(2)}, u32[]{:S(2)}) async-start(bf16[8,2,32768]{2,1,0:T(2,128)(2,1)} %reshape.95), calls=%async_computation | async-start | bytes 2097152 | tf_op jit(solution)/shard_map/all_to_all | solution.py:105
  45.8 11.5 %copy-start.7 = (bf16[1,4,32,512]{3,2,1,0:T(8,128)(2,1)S(1)}, bf16[1,4,32,512]{3,2,1,0:T(8,128)(2,1)}, u32[]{:S(2)}) copy-start(bf16[1,4,32,512]{3,2,1,0:T(8,128)(2,1)} %param.20) | copy-start | bytes 393220
  45.8 33.7 %all-gather.2.cloned.1.call-start = ((), (), s32[]{:S(2)}) async-start(), calls=%async_computation.1 | async-start | bytes 1179648 | tf_op jit(solution)/shard_map/all_gather | solution.py:108
  46.6 12.0 %copy-start.9 = (u32[32]{0:T(128)S(1)}, u32[32]{0:T(128)}, u32[]{:S(2)}) copy-start(u32[32]{0:T(128)} %constant.56) | copy-start | bytes 388
  46.6 13.3 %copy-start.8 = (s32[8]{0:T(128)S(1)}, s32[8]{0:T(128)}, u32[]{:S(2)}) copy-start(s32[8]{0:T(128)} %param.14) | copy-start | bytes 100
  46.9 8.7 %collective-permute-start.1 = (bf16[4,32,512]{2,1,0:T(8,128)(2,1)S(1)}, bf16[4,32,512]{2,1,0:T(8,128)(2,1)S(1)}, u32[]{:S(2)}, u32[]{:S(2)}) collective-permute-start(bf16[4,32,512]{2,1,0:T(8,128)(2,1)S(1)} %add_convert_fusion.1), channel_id=1, source_target_pairs={{8,0},{16,8},{24,16},{9,1},{17,9},{25,17},{10,2},{18,10},{26,18},{... | collective-permute-start | bytes 393224 | tf_op jit(solution)/shard_map/ppermute | solution.py:18
  55.8 7.4 %collective-permute-start.2 = (bf16[4,32,512]{2,1,0:T(8,128)(2,1)S(1)}, bf16[4,32,512]{2,1,0:T(8,128)(2,1)S(1)}, u32[]{:S(2)}, u32[]{:S(2)}) collective-permute-start(bf16[4,32,512]{2,1,0:T(8,128)(2,1)S(1)} %add_convert_fusion), channel_id=1, source_target_pairs={{8,0},{16,8},{24,16},{9,1},{17,9},{25,17},{10,2},{18,10},{26,18},{... | collective-permute-start | bytes 393224 | tf_op jit(solution)/shard_map/ppermute | solution.py:18
  63.5 3.2 %copy-start.6 = (bf16[1,1,512,512]{3,2,1,0:T(8,128)(2,1)S(1)}, bf16[1,1,512,512]{3,2,1,0:T(8,128)(2,1)}, u32[]{:S(2)}) copy-start(bf16[1,1,512,512]{3,2,1,0:T(8,128)(2,1)} %param.15) | copy-start | bytes 1572868
  79.5 2.5 %copy-start.2 = (bf16[4,512,512]{2,0,1:T(4,128)(2,1)S(1)}, bf16[4,512,512]{2,0,1:T(4,128)(2,1)}, u32[]{:S(2)}) copy-start(bf16[4,512,512]{2,0,1:T(4,128)(2,1)} %get-tuple-element.112) | copy-start | bytes 6291460 | tf_op jit(solution)/shard_map/while
  85.9 2.5 %copy-start.2 = (bf16[4,512,512]{2,0,1:T(4,128)(2,1)S(1)}, bf16[4,512,512]{2,0,1:T(4,128)(2,1)}, u32[]{:S(2)}) copy-start(bf16[4,512,512]{2,0,1:T(4,128)(2,1)} %get-tuple-element.112) | copy-start | bytes 6291460 | tf_op jit(solution)/shard_map/while
Sparse Core Ops, SparseCore 0:
  48.5 26.8 all-gather.1
where the time goes:
time: 126 us; the launch traced here: 125 us
  other arithmetic  24.9 us (20%)
  blocking collectives  24.2 us (19%)
  matrix products  22.4 us (18%)
  local copies, waits for them, and re-layouts  19.1 us (15%)
  between operations  14.3 us (11%)
  waiting for transfers between devices  10.6 us (8%)
  starting transfers between devices  9.43 us (7%)
    unnamed x1, other arithmetic  23.4 us
    unnamed x25, local copies, waits for them, and re-layouts  13.9 us
    unnamed x1, blocking collectives  13.1 us
    psum x1, blocking collectives, body(): mine = lax.psum(mine, 'seg')  11.2 us
    ppermute x3, waiting for transfers between devices, passed_along(): lax.ppermute(value, axis, [(source, source + steps) for source in range(f...  9.91 us
    dot_general x2, matrix products, one_batch(): jnp.einsum('bde,qde->bq', outer_prod, precond, preferred_element_type=jnp...  7.62 us
    all_to_all x1, starting transfers between devices, body(): lax.all_to_all(train_grads, 'blk', split_axis=2, concat_axis=1, tiled=True)  5.33 us
    dot_general x2, matrix products, one_batch(): jnp.einsum('btd,bte->bde', grad_block, act_block, preferred_element_type=...  4.98 us
  transfers between devices with their start and end apart: 5, of which 2 were waited for; matrix products, arithmetic and copies ran while one was open for 40% of the time, Pallas kernels for 0%

commit v1 on v0

v1 whole, which is shorter than its diff:
```python
import functools

import jax
import jax.numpy as jnp
from jax import lax
from jax.experimental import pallas as pl
from jax.experimental.pallas import tpu as pltpu
from jax.sharding import PartitionSpec as P

SLOTS = 2
damping = 0.05
F32 = jnp.float32
B16 = jnp.bfloat16
MESH = pl.DeviceIdType.MESH


def kernel(
    segs,
    blks,
    queries,
    counts,
    acts_h,
    grads_h,
    bin_h,
    bout_h,
    eig_h,
    back_h,
    deriv_h,
    qacts_h,
    qtop_h,
    out,
    acts,
    own_g,
    other_g,
    other_a,
    b_in,
    b_out,
    eig,
    back,
    deriv,
    qacts,
    errs,
    moved,
    inv,
    rot_q,
    core_all,
    grads,
    racts,
    part,
    part_in,
    zsum,
    load_sem,
    sel_send,
    sel_recv,
    g0_send,
    g0_recv,
    g1_send,
    g1_recv,
    a_send,
    a_recv,
    f_send,
    e_send,
    e_recv,
    p_send,
    p_recv,
    z_send,
    z_recv,
):
    seg = lax.axis_index("seg")
    blk = lax.axis_index("blk")
    chips = blks // 2
    chip = blk // 2
    lane = blk % 2
    mate_lane = 1 - lane
    mate = chip * 2 + mate_lane
    rows = acts_h.shape[0]
    tb = rows // SLOTS
    half = tb // 2
    per = tb + half
    width = bin_h.shape[0]
    qt = qtop_h.shape[0] // queries

    def remote(src, dst, ssem, rsem, seg_to, blk_to):
        return pltpu.make_async_remote_copy(
            src_ref=src,
            dst_ref=dst,
            send_sem=ssem,
            recv_sem=rsem,
            device_id=(seg_to, blk_to),
            device_id_type=MESH,
        )

    def cols(index):
        return pl.ds(pl.multiple_of(index * width, width), width)

    barrier = pltpu.get_barrier_semaphore()
    for off in range(1, blks):
        pl.semaphore_signal(
            barrier, inc=1, device_id=(seg, lax.rem(blk + off, blks)), device_id_type=MESH
        )
    for off in range(1, segs):
        pl.semaphore_signal(
            barrier, inc=1, device_id=(lax.rem(seg + off, segs), blk), device_id_type=MESH
        )

    keep = pl.ds(pl.multiple_of(tb + lane * half, half), half)
    give = pl.ds(pl.multiple_of(tb + mate_lane * half, half), half)
    mine0 = pl.ds(pl.multiple_of(lane * per, half), tb)
    mine1 = pl.ds(pl.multiple_of(lane * per + tb, half), half)
    mine = pl.ds(pl.multiple_of(lane * per, half), per)
    theirs = pl.ds(pl.multiple_of(mate_lane * per, half), per)

    loads = [
        pltpu.make_async_copy(src, dst, load_sem.at[n])
        for n, (src, dst) in enumerate(
            (
                (back_h, back),
                (deriv_h, deriv),
                (acts_h, acts),
                (bin_h, b_in),
                (grads_h.at[keep, :], own_g),
                (qacts_h, qacts),
                (eig_h, eig),
                (bout_h, b_out),
            )
        )
    ]
    l_back, l_deriv, l_acts, l_bin, l_own, l_qacts, l_eig, l_bout = loads
    l_top = pltpu.make_async_copy(qtop_h, errs, load_sem.at[len(loads)])

    @pl.when(seg == segs - 1)
    def _():
        l_top.start()

    for load in loads:
        load.start()
    own0 = pltpu.make_async_copy(
        grads_h.at[pl.ds(0, tb), cols(blk)], grads.at[0, mine0], g0_recv.at[0, lane]
    )
    own0.start()

    pl.semaphore_wait(barrier, blks - 1 + segs - 1)

    sel_a = remote(acts_h.at[give, :], other_a, sel_send.at[0], sel_recv.at[0], seg, mate)
    sel_a.start()
    sel_g = remote(grads_h.at[give, :], other_g, sel_send.at[1], sel_recv.at[1], seg, mate)
    sel_g.start()
    sends = [sel_a, sel_g]

    def to_chip(off):
        return lax.rem(chip + off, chips)

    def targets():
        for off in range(1, chips):
            for side in range(2):
                yield off, side, to_chip(off) * 2 + side
        yield 0, 0, mate

    for off, side, dest in targets():
        copy = remote(
            grads_h.at[pl.ds(0, tb), cols(dest)],
            grads.at[off, mine0],
            g0_send.at[off, side],
            g0_recv.at[off, lane],
            seg,
            dest,
        )
        copy.start()
        sends.append(copy)

    def e_copy(q):
        r = pl.ds(q * qt, qt)
        return remote(
            moved.at[r],
            errs.at[r],
            e_send.at[q],
            e_recv.at[q],
            lax.rem(seg + segs - 1, segs),
            blk,
        )

    def advance(q):
        r = pl.ds(q * qt, qt)
        e = errs[r]
        mixed = jnp.dot(e, back[...], preferred_element_type=F32)
        moved[r] = (e.astype(F32) + mixed * deriv[r].astype(F32)).astype(B16)
        e_copy(q).start()

    l_back.wait()
    l_deriv.wait()

    @pl.when(seg == segs - 1)
    def _():
        l_top.wait()
        for q in range(queries):
            advance(q)

    full = counts[blk] == SLOTS
    l_acts.wait()
    l_bin.wait()
    sel_a.wait_recv()
    racts[0, mine0] = jnp.dot(acts[0:tb], b_in[...], preferred_element_type=F32).astype(B16)
    picked = jnp.where(full, acts[keep, :].astype(F32), other_a[...].astype(F32)).astype(B16)
    racts[0, mine1] = jnp.dot(picked, b_in[...], preferred_element_type=F32).astype(B16)
    for off in list(range(1, chips)) + [0]:
        dest = mate if off == 0 else to_chip(off) * 2 + lane
        copy = remote(
            racts.at[0, mine], racts.at[off, mine], a_send.at[off], a_recv.at[off, lane], seg, dest
        )
        copy.start()
        sends.append(copy)

    l_own.wait()
    sel_g.wait_recv()
    own_g[...] = jnp.where(full, own_g[...].astype(F32), other_g[...].astype(F32)).astype(B16)
    for off, side, dest in targets():
        copy = remote(
            own_g.at[:, cols(dest)],
            grads.at[off, mine1],
            g1_send.at[off, side],
            g1_recv.at[off, lane],
            seg,
            dest,
        )
        copy.start()
        sends.append(copy)
    own1 = pltpu.make_async_copy(own_g.at[:, cols(blk)], grads.at[0, mine1], g1_recv.at[0, lane])
    own1.start()

    l_qacts.wait()
    rot_q[...] = jnp.dot(qacts[...], b_in[...], preferred_element_type=F32).astype(B16)
    l_eig.wait()
    inv[...] = 1.0 / (eig[...].astype(F32) + damping)
    l_bout.wait()

    @pl.when(jnp.logical_and(seg > 0, seg < segs - 1))
    def _():
        for q in range(queries):
            e_copy(q).wait_recv()
            advance(q)

    for off in range(1, chips):
        remote(
            racts.at[off, mine], racts.at[off, mine], f_send.at[off], a_recv.at[off, lane], seg, mate
        ).wait_recv()
        copy = remote(
            racts.at[off, mine], racts.at[off, mine], f_send.at[off], a_recv.at[off, lane], seg, mate
        )
        copy.start()
        sends.append(copy)

    @pl.when(seg == 0)
    def _():
        for q in range(queries):
            e_copy(q).wait_recv()

    rot_e = jnp.dot(errs[...], b_out[...], preferred_element_type=F32).astype(B16)
    for q in range(queries):
        raw = lax.dot_general(
            rot_e[q * qt : (q + 1) * qt],
            rot_q[q * qt : (q + 1) * qt, :],
            (((0,), (0,)), ((), ())),
            preferred_element_type=F32,
        )
        core_all[:, q * width : (q + 1) * width] = (raw * inv[...]).astype(B16)

    def group(i, carry):
        for side in range(2):
            for sem, size in ((g0_recv, tb), (g1_recv, half)):
                ref = grads.at[i, pl.ds(side * per + (tb if size == half else 0), size)]
                remote(ref, ref, g0_send.at[0, 0], sem.at[i, side], seg, mate).wait_recv()
        ref = racts.at[i, theirs]
        remote(ref, ref, f_send.at[0], a_recv.at[i, mate_lane], seg, mate).wait_recv()
        turned = jnp.dot(grads[i], b_out[...], preferred_element_type=F32).astype(B16)
        at = racts[i].astype(F32)
        for q in range(queries):
            h = jnp.dot(
                turned,
                core_all[:, q * width : (q + 1) * width],
                preferred_element_type=F32,
            )
            prod = h * at

            def small(x):
                x = jnp.sum(x, axis=0, keepdims=True)
                return sum(x[:, n * 128 : (n + 1) * 128] for n in range(width // 128))

            shared = small(prod[tb:per] + prod[per + tb : 2 * per])
            for side in range(2):
                part[i, side, q : q + 1, :] = small(prod[side * per : side * per + tb])
                part[i, side, queries + q : queries + q + 1, :] = shared
        return carry

    lax.fori_loop(0, chips, group, 0)

    def back_targets():
        for off in range(1, chips):
            for side in range(2):
                yield off, side, lax.rem(chip + chips - off, chips) * 2 + side

    for off, side, dest in back_targets():
        copy = remote(
            part.at[off, side],
            part_in.at[off, lane],
            p_send.at[off, side],
            p_recv.at[off, lane],
            seg,
            dest,
        )
        copy.start()
        sends.append(copy)
    copy = remote(
        part.at[0, mate_lane], part_in.at[0, lane], p_send.at[0, 0], p_recv.at[0, lane], seg, mate
    )
    copy.start()
    sends.append(copy)

    def p_wait(off, side):
        ref = part_in.at[off, side]
        remote(ref, ref, p_send.at[0, 0], p_recv.at[off, side], seg, mate).wait_recv()

    p_wait(0, mate_lane)
    total = part[0, lane] + part_in[0, mate_lane]
    for off in range(1, chips):
        for side in range(2):
            p_wait(off, side)
            total = total + part_in[off, side]
    zsum[seg] = total
    for off in range(1, segs):
        copy = remote(
            zsum.at[seg], zsum.at[seg], z_send.at[off], z_recv.at[seg], lax.rem(seg + off, segs), blk
        )
        copy.start()
        sends.append(copy)
    for off in range(1, segs):
        source = lax.rem(seg + off, segs)
        ref = zsum.at[source]
        remote(ref, ref, z_send.at[off], z_recv.at[source], source, blk).wait_recv()
    total = zsum[0]
    for n in range(1, segs):
        total = total + zsum[n]
    total = jnp.sum(total, axis=1, keepdims=True)
    out[:, 0:1] = total[0:queries]
    out[:, 1:2] = total[queries : 2 * queries] * jnp.where(full, 1.0, 0.0)

    for copy in sends:
        copy.wait_send()

    @pl.when(seg > 0)
    def _():
        for q in range(queries):
            e_copy(q).wait_send()


def body(
    train_acts,
    train_grads,
    counts,
    basis_in,
    basis_out,
    eigenvalues,
    back_weight,
    derivative,
    query_acts,
    query_top,
):
    segs = lax.axis_size("seg")
    blks = lax.axis_size("blk")
    chips = blks // 2
    queries, qt, width = query_top.shape
    rows = train_acts.shape[1]
    half = rows // SLOTS // 2
    per = rows // SLOTS + half
    wide = train_grads.shape[2]
    any_spec = pl.BlockSpec(memory_space=pl.ANY)
    vm = pltpu.VMEM
    dma = pltpu.SemaphoreType.DMA
    return pl.pallas_call(
        functools.partial(kernel, segs, blks, queries),
        out_shape=jax.ShapeDtypeStruct((queries, SLOTS), F32),
        in_specs=[pl.BlockSpec(memory_space=pltpu.SMEM)] + [any_spec] * 9,
        out_specs=pl.BlockSpec(memory_space=pltpu.VMEM),
        scratch_shapes=[
            vm((rows, width), B16),
            vm((half, wide), B16),
            vm((half, wide), B16),
            vm((half, width), B16),
            vm((width, width), B16),
            vm((width, width), B16),
            vm((width, width), B16),
            vm((width, width), B16),
            vm((queries * qt, width), B16),
            vm((queries * qt, width), B16),
            vm((queries * qt, width), B16),
            vm((queries * qt, width), B16),
            vm((width, width), F32),
            vm((queries * qt, width), B16),
            vm((width, queries * width), B16),
            vm((chips, 2 * per, width), B16),
            vm((chips, 2 * per, width), B16),
            vm((chips, 2, 2 * queries, 128), F32),
            vm((chips, 2, 2 * queries, 128), F32),
            vm((segs, 2 * queries, 128), F32),
            dma((9,)),
            dma((2,)),
            dma((2,)),
            dma((chips, 2)),
            dma((chips, 2)),
            dma((chips, 2)),
            dma((chips, 2)),
            dma((chips,)),
            dma((chips, 2)),
            dma((chips,)),
            dma((queries,)),
            dma((queries,)),
            dma((chips, 2)),
            dma((chips, 2)),
            dma((segs,)),
            dma((segs,)),
        ],
        compiler_params=pltpu.CompilerParams(
            collective_id=0, has_side_effects=True, vmem_limit_bytes=40 * 1024 * 1024
        ),
    )(
        counts,
        train_acts[0],
        train_grads[0],
        basis_in[0, 0],
        basis_out[0, 0],
        eigenvalues[0, 0],
        back_weight[0, 0],
        derivative[0].reshape(queries * qt, width),
        query_acts[0].reshape(queries * qt, width),
        query_top.reshape(queries * qt, width),
    )


def solution(mesh):
    in_specs = (
        P("seg", "blk", None),
        P("seg", "blk", None),
        P(),
        P("seg", None, None, None),
        P("seg", "blk", None, None),
        P("seg", "blk", None, None),
        P("seg", "blk", None, None),
        P("seg", None, None, "blk"),
        P("seg", None, None, None),
        P(None, None, "blk"),
    )
    out_specs = P(None, "blk")
    return jax.shard_map(body, mesh=mesh, in_specs=in_specs, out_specs=out_specs, check_vma=False)
```

time: 126 us -> 41.6 us (0.33)
  Pallas kernels: 0 us -> 30.9 us
  other arithmetic: 24.9 us -> 0 us
  blocking collectives: 24.2 us -> 0 us
  matrix products: 22.4 us -> 0 us
  between operations: 14.3 us -> 0.02 us
  waiting for transfers between devices: 10.6 us -> 0 us
  starting transfers between devices: 9.43 us -> 0 us
  local copies, waits for them, and re-layouts: 19.1 us -> 10.3 us
    pallas_call x0 -> x1, Pallas kernels: none -> 30.9 us  [body(): pl.pallas_call(functools.partial(kernel, segs, blks, queries), out_shape=...]
    unnamed x1 -> x0, other arithmetic: 23.4 us -> none
    dot_general x12 -> x0, matrix products: 22.4 us -> none  [the longest x2 7.62 us: one_batch(): jnp.einsum('bde,qde->bq', outer_prod, precond, preferred_element_type=jnp...]
    unnamed x1 -> x0, blocking collectives: 13.1 us -> none
    psum x1 -> x0, blocking collectives: 11.2 us -> none  [body(): mine = lax.psum(mine, 'seg')]
    ppermute x3 -> x0, waiting for transfers between devices: 9.91 us -> none  [passed_along(): lax.ppermute(value, axis, [(source, source + steps) for source in range(f...]
    all_to_all x1 -> x0, starting transfers between devices: 5.33 us -> none  [body(): lax.all_to_all(train_grads, 'blk', split_axis=2, concat_axis=1, tiled=True)]
    unnamed x25 -> x20, local copies, waits for them, and re-layouts: 13.9 us -> 9.66 us
  transfers between devices with their start and end apart: 5 -> 0, of which waited for: 2 -> 0; matrix products, arithmetic and copies ran while one was open for 40% -> 0% of each run, Pallas kernels for 0% -> 0%
where the time goes in v1:
time: 41.6 us; the launch traced here: 41.2 us
  Pallas kernels  30.9 us (74%)
  local copies, waits for them, and re-layouts  10.3 us (25%)
    pallas_call x1, Pallas kernels, body(): pl.pallas_call(functools.partial(kernel, segs, blks, queries), out_shape=...  30.9 us
    unnamed x20, local copies, waits for them, and re-layouts  9.66 us

profile of v1, /device:TPU:0, one launch (start us, length us, event | category | flops | bytes accessed | tf_op | source)
XLA Modules:
  0.0 41.2 jit_solution(17000605044162476139)
XLA Ops:
  0.0 0.0 copy-start.9
  0.0 0.7 %copy-done.9 = s32[8]{0:T(128)S(1)} copy-done((s32[8]{0:T(128)S(1)}, s32[8]{0:T(128)}, u32[]{:S(2)}) %copy-start.9) | copy-done | bytes 56
  0.7 0.0 copy-start
  0.7 1.2 %copy-done = bf16[1,128,4096]{2,1,0:T(8,128)(2,1)S(1)} copy-done((bf16[1,128,4096]{2,1,0:T(8,128)(2,1)S(1)}, bf16[1,128,4096]{2,1,0:T(8,128)(2,1)}, u32[]{:S(2)}) %copy-start) | copy-done | bytes 1048600
  1.9 0.0 copy-start.1
  1.9 1.0 %copy-done.1 = bf16[1,1,512,512]{3,2,1,0:T(8,128)(2,1)S(1)} copy-done((bf16[1,1,512,512]{3,2,1,0:T(8,128)(2,1)S(1)}, bf16[1,1,512,512]{3,2,1,0:T(8,128)(2,1)}, u32[]{:S(2)}) %copy-start.1) | copy-done | bytes 524312
  2.9 0.0 copy-start.2
  2.9 1.0 %copy-done.2 = bf16[1,1,512,512]{3,2,1,0:T(8,128)(2,1)S(1)} copy-done((bf16[1,1,512,512]{3,2,1,0:T(8,128)(2,1)S(1)}, bf16[1,1,512,512]{3,2,1,0:T(8,128)(2,1)}, u32[]{:S(2)}) %copy-start.2) | copy-done | bytes 524312
  4.0 0.0 copy-start.3
  4.0 1.0 %copy-done.3 = bf16[1,1,512,512]{3,2,1,0:T(8,128)(2,1)S(1)} copy-done((bf16[1,1,512,512]{3,2,1,0:T(8,128)(2,1)S(1)}, bf16[1,1,512,512]{3,2,1,0:T(8,128)(2,1)}, u32[]{:S(2)}) %copy-start.3) | copy-done | bytes 524312
  5.0 0.0 copy-start.4
  5.0 1.0 %copy-done.4 = bf16[1,1,512,512]{3,2,1,0:T(8,128)(2,1)S(1)} copy-done((bf16[1,1,512,512]{3,2,1,0:T(8,128)(2,1)S(1)}, bf16[1,1,512,512]{3,2,1,0:T(8,128)(2,1)}, u32[]{:S(2)}) %copy-start.4) | copy-done | bytes 524312
  6.0 0.0 copy-start.5
  6.1 0.9 %copy-done.5 = bf16[1,128,512]{2,1,0:T(8,128)(2,1)S(1)} copy-done((bf16[1,128,512]{2,1,0:T(8,128)(2,1)S(1)}, bf16[1,128,512]{2,1,0:T(8,128)(2,1)}, u32[]{:S(2)}) %copy-start.5) | copy-done | bytes 131096
  7.0 0.0 copy-start.6
  7.0 0.9 %copy-done.6 = bf16[1,4,32,512]{3,2,1,0:T(8,128)(2,1)S(1)} copy-done((bf16[1,4,32,512]{3,2,1,0:T(8,128)(2,1)S(1)}, bf16[1,4,32,512]{3,2,1,0:T(8,128)(2,1)}, u32[]{:S(2)}) %copy-start.6) | copy-done | bytes 131096
  7.9 0.0 copy-start.7
  7.9 0.9 %copy-done.7 = bf16[1,4,32,512]{3,2,1,0:T(8,128)(2,1)S(1)} copy-done((bf16[1,4,32,512]{3,2,1,0:T(8,128)(2,1)S(1)}, bf16[1,4,32,512]{3,2,1,0:T(8,128)(2,1)}, u32[]{:S(2)}) %copy-start.7) | copy-done | bytes 131096
  8.8 0.0 copy-start.8
  8.8 0.9 %copy-done.8 = bf16[4,32,512]{2,1,0:T(8,128)(2,1)S(1)} copy-done((bf16[4,32,512]{2,1,0:T(8,128)(2,1)S(1)}, bf16[4,32,512]{2,1,0:T(8,128)(2,1)}, u32[]{:S(2)}) %copy-start.8) | copy-done | bytes 131096
  9.7 30.9 %shard_map.100 = f32[4,2]{1,0:T(4,128)S(1)} custom-call(s32[8]{0:T(128)S(1)} %copy-done.9, bf16[128,512]{1,0:T(8,128)(2,1)S(1)} %bitcast.14, bf16[128,4096]{1,0:T(8,128)(2,1)S(1)} %bitcast.9, bf16[512,512]{1,0:T(8,128)(2,1)S(1)} %bitcast.10, bf16[512,512]{1,0:T(8,128)(2,1)S(1)} %bitcast.11, bf16[512,512]{1,0:T(8,128)(2,1)S(1)} %bitcast.12, ...), custom_call_target="tpu_custom_call" | custom-call | tf_op jit(solution)/shard_map/pallas_call | solution.py:378
  40.5 0.6 %copy.11 = f32[4,2]{0,1:T(2,128)} copy(f32[4,2]{1,0:T(4,128)S(1)} %shard_map.100) | data formatting | bytes 64 | tf_op jit(solution)/shard_map/pallas_call | solution.py:378
Async XLA Ops:
  0.0 0.7 %copy-start.9 = (s32[8]{0:T(128)S(1)}, s32[8]{0:T(128)}, u32[]{:S(2)}) copy-start(s32[8]{0:T(128)} %counts.1) | copy-start | bytes 100
  0.7 1.2 %copy-start = (bf16[1,128,4096]{2,1,0:T(8,128)(2,1)S(1)}, bf16[1,128,4096]{2,1,0:T(8,128)(2,1)}, u32[]{:S(2)}) copy-start(bf16[1,128,4096]{2,1,0:T(8,128)(2,1)} %param.11) | copy-start | bytes 3145732
  1.9 1.0 %copy-start.1 = (bf16[1,1,512,512]{3,2,1,0:T(8,128)(2,1)S(1)}, bf16[1,1,512,512]{3,2,1,0:T(8,128)(2,1)}, u32[]{:S(2)}) copy-start(bf16[1,1,512,512]{3,2,1,0:T(8,128)(2,1)} %param.13) | copy-start | bytes 1572868
  2.9 1.0 %copy-start.2 = (bf16[1,1,512,512]{3,2,1,0:T(8,128)(2,1)S(1)}, bf16[1,1,512,512]{3,2,1,0:T(8,128)(2,1)}, u32[]{:S(2)}) copy-start(bf16[1,1,512,512]{3,2,1,0:T(8,128)(2,1)} %param.14) | copy-start | bytes 1572868
  4.0 1.0 %copy-start.3 = (bf16[1,1,512,512]{3,2,1,0:T(8,128)(2,1)S(1)}, bf16[1,1,512,512]{3,2,1,0:T(8,128)(2,1)}, u32[]{:S(2)}) copy-start(bf16[1,1,512,512]{3,2,1,0:T(8,128)(2,1)} %param.15) | copy-start | bytes 1572868
  5.0 1.0 %copy-start.4 = (bf16[1,1,512,512]{3,2,1,0:T(8,128)(2,1)S(1)}, bf16[1,1,512,512]{3,2,1,0:T(8,128)(2,1)}, u32[]{:S(2)}) copy-start(bf16[1,1,512,512]{3,2,1,0:T(8,128)(2,1)} %param.16) | copy-start | bytes 1572868
  6.0 0.9 %copy-start.5 = (bf16[1,128,512]{2,1,0:T(8,128)(2,1)S(1)}, bf16[1,128,512]{2,1,0:T(8,128)(2,1)}, u32[]{:S(2)}) copy-start(bf16[1,128,512]{2,1,0:T(8,128)(2,1)} %param.10) | copy-start | bytes 393220
  7.0 0.9 %copy-start.6 = (bf16[1,4,32,512]{3,2,1,0:T(8,128)(2,1)S(1)}, bf16[1,4,32,512]{3,2,1,0:T(8,128)(2,1)}, u32[]{:S(2)}) copy-start(bf16[1,4,32,512]{3,2,1,0:T(8,128)(2,1)} %param.17) | copy-start | bytes 393220
  7.9 0.9 %copy-start.7 = (bf16[1,4,32,512]{3,2,1,0:T(8,128)(2,1)S(1)}, bf16[1,4,32,512]{3,2,1,0:T(8,128)(2,1)}, u32[]{:S(2)}) copy-start(bf16[1,4,32,512]{3,2,1,0:T(8,128)(2,1)} %param.18) | copy-start | bytes 393220
  8.8 0.9 %copy-start.8 = (bf16[4,32,512]{2,1,0:T(8,128)(2,1)S(1)}, bf16[4,32,512]{2,1,0:T(8,128)(2,1)}, u32[]{:S(2)}) copy-start(bf16[4,32,512]{2,1,0:T(8,128)(2,1)} %param.19) | copy-start | bytes 393220

commit v2 on v1

--- a/solution.py
+++ b/solution.py
@@ -372,7 +372,7 @@
     half = rows // SLOTS // 2
     per = rows // SLOTS + half
     wide = train_grads.shape[2]
-    any_spec = pl.BlockSpec(memory_space=pl.ANY)
+    any_spec = pl.BlockSpec(memory_space=pltpu.HBM)
     vm = pltpu.VMEM
     dma = pltpu.SemaphoreType.DMA
     return pl.pallas_call(
@@ -419,7 +419,7 @@
             dma((segs,)),
         ],
         compiler_params=pltpu.CompilerParams(
-            collective_id=0, has_side_effects=True, vmem_limit_bytes=40 * 1024 * 1024
+            collective_id=0, has_side_effects=True, vmem_limit_bytes=67_043_328
         ),
     )(
         counts,

time: 41.6 us -> 33.3 us (0.80)
  local copies, waits for them, and re-layouts: 10.3 us -> 1.32 us
  Pallas kernels: 30.9 us -> 31.8 us
    unnamed x20 -> x0, local copies, waits for them, and re-layouts: 9.66 us -> none
    pallas_call x1, Pallas kernels: 30.9 us -> 31.8 us  [body(): pl.pallas_call(functools.partial(kernel, segs, blks, queries), out_shape=...]
    pallas_call x1, local copies, waits for them, and re-layouts: 0.65 us -> 1.32 us  [body(): pl.pallas_call(functools.partial(kernel, segs, blks, queries), out_shape=...]
where the time goes in v2:
time: 33.3 us; the launch traced here: 33.1 us
  Pallas kernels  31.8 us (95%)
  local copies, waits for them, and re-layouts  1.32 us (4%)
    pallas_call x1, Pallas kernels, body(): pl.pallas_call(functools.partial(kernel, segs, blks, queries), out_shape=...  31.8 us
    pallas_call x1, local copies, waits for them, and re-layouts, body(): pl.pallas_call(functools.partial(kernel, segs, blks, queries), out_shape=...  1.32 us

profile of v2, /device:TPU:0, one launch (start us, length us, event | category | flops | bytes accessed | tf_op | source)
XLA Modules:
  0.0 33.1 jit_solution(6518362641439711689)
XLA Ops:
  0.0 31.8 %shard_map.100 = f32[4,2]{1,0:T(4,128)} custom-call(s32[8]{0:T(128)} %counts.1, bf16[128,512]{1,0:T(8,128)(2,1)} %bitcast.14, bf16[128,4096]{1,0:T(8,128)(2,1)} %bitcast.9, bf16[512,512]{1,0:T(8,128)(2,1)} %bitcast.10, bf16[512,512]{1,0:T(8,128)(2,1)} %bitcast.11, bf16[512,512]{1,0:T(8,128)(2,1)} %bitcast.12, bf16[512,512]{1,0:T(8,128)(2,1)} %bitcast.13, ...), custom_call_target="tpu_custom_call" | custom-call | tf_op jit(solution)/shard_map/pallas_call | solution.py:378
  31.8 1.3 %copy.11 = f32[4,2]{0,1:T(2,128)} copy(f32[4,2]{1,0:T(4,128)} %shard_map.100) | data formatting | bytes 64 | tf_op jit(solution)/shard_map/pallas_call | solution.py:378

commit v3 on v2

v3 whole, which is shorter than its diff:
```python
import functools

import jax
import jax.numpy as jnp
from jax import lax
from jax.experimental import pallas as pl
from jax.experimental.pallas import tpu as pltpu
from jax.sharding import PartitionSpec as P

SLOTS = 2
damping = 0.05
F32 = jnp.float32
B16 = jnp.bfloat16
MESH = pl.DeviceIdType.MESH


def kernel(
    segs,
    blks,
    queries,
    counts,
    acts_h,
    grads_h,
    bin_h,
    bout_h,
    eig_h,
    back_h,
    deriv_h,
    qacts_h,
    qtop_h,
    out,
    acts,
    own_g,
    other_g,
    other_a,
    b_in,
    b_out,
    eig,
    back,
    deriv,
    qacts,
    errs,
    moved,
    inv,
    rot_q,
    core_all,
    grads0,
    grads1,
    racts0,
    racts1,
    turned0,
    part,
    packed,
    gathered,
    load_sem,
    sel_send,
    sel_recv,
    g0_send,
    g0_recv,
    g1_send,
    g1_recv,
    a0_send,
    a0_recv,
    a1_send,
    a1_recv,
    f0_send,
    f1_send,
    e_send,
    e_recv,
    p_send,
    p_recv,
    ready,
):
    seg = lax.axis_index("seg")
    blk = lax.axis_index("blk")
    chips = blks // 2
    chip = blk // 2
    lane = blk % 2
    mate_lane = 1 - lane
    mate = chip * 2 + mate_lane
    rows = acts_h.shape[0]
    tb = rows // SLOTS
    half = tb // 2
    width = bin_h.shape[0]
    qt = qtop_h.shape[0] // queries

    def remote(src, dst, ssem, rsem, seg_to, blk_to):
        return pltpu.make_async_remote_copy(
            src_ref=src,
            dst_ref=dst,
            send_sem=ssem,
            recv_sem=rsem,
            device_id=(seg_to, blk_to),
            device_id_type=MESH,
        )

    def cols(index):
        return pl.ds(pl.multiple_of(index * width, width), width)

    barrier = pltpu.get_barrier_semaphore()
    for off in range(1, blks):
        pl.semaphore_signal(
            barrier, inc=1, device_id=(seg, lax.rem(blk + off, blks)), device_id_type=MESH
        )
    for off in range(1, segs):
        pl.semaphore_signal(
            barrier, inc=1, device_id=(lax.rem(seg + off, segs), blk), device_id_type=MESH
        )

    keep = pl.ds(pl.multiple_of(tb + lane * half, half), half)
    give = pl.ds(pl.multiple_of(tb + mate_lane * half, half), half)
    mine0 = pl.ds(pl.multiple_of(lane * tb, tb), tb)
    mine1 = pl.ds(pl.multiple_of(lane * half, half), half)

    loads = [
        pltpu.make_async_copy(src, dst, load_sem.at[n])
        for n, (src, dst) in enumerate(
            (
                (back_h, back),
                (deriv_h, deriv),
                (acts_h, acts),
                (bin_h, b_in),
                (grads_h.at[keep, :], own_g),
                (qacts_h, qacts),
                (eig_h, eig),
                (bout_h, b_out),
            )
        )
    ]
    l_back, l_deriv, l_acts, l_bin, l_own, l_qacts, l_eig, l_bout = loads
    l_top = pltpu.make_async_copy(qtop_h, errs, load_sem.at[len(loads)])

    @pl.when(seg == segs - 1)
    def _():
        l_top.start()

    for load in loads:
        load.start()
    own0 = pltpu.make_async_copy(
        grads_h.at[pl.ds(0, tb), cols(blk)], grads0.at[0, mine0], g0_recv.at[0, lane]
    )
    own0.start()

    def e_copy(q):
        r = pl.ds(q * qt, qt)
        return remote(
            moved.at[r],
            errs.at[r],
            e_send.at[q],
            e_recv.at[q],
            lax.rem(seg + segs - 1, segs),
            blk,
        )

    def advance(q):
        r = pl.ds(q * qt, qt)
        e = errs[r]
        mixed = jnp.dot(e, back[...], preferred_element_type=F32)
        moved[r] = (e.astype(F32) + mixed * deriv[r].astype(F32)).astype(B16)

    l_back.wait()
    l_deriv.wait()

    @pl.when(seg == segs - 1)
    def _():
        l_top.wait()
        for q in range(queries):
            advance(q)

    l_acts.wait()
    l_bin.wait()
    racts0[0, mine0] = jnp.dot(acts[0:tb], b_in[...], preferred_element_type=F32).astype(B16)

    pl.semaphore_wait(barrier, blks - 1 + segs - 1)

    @pl.when(seg == segs - 1)
    def _():
        for q in range(queries):
            e_copy(q).start()

    sends = []

    def send(copy):
        copy.start()
        sends.append(copy)
        return copy

    sel_a = send(remote(acts_h.at[give, :], other_a, sel_send.at[0], sel_recv.at[0], seg, mate))
    sel_g = send(remote(grads_h.at[give, :], other_g, sel_send.at[1], sel_recv.at[1], seg, mate))

    def to_chip(off):
        return lax.rem(chip + off, chips)

    def targets():
        for off in range(1, chips):
            for side in range(2):
                yield off, side, to_chip(off) * 2 + side
        yield 0, 0, mate

    def act_targets():
        for off in range(1, chips):
            yield off, to_chip(off) * 2 + lane
        yield 0, mate

    for off, side, dest in targets():
        send(
            remote(
                grads_h.at[pl.ds(0, tb), cols(dest)],
                grads0.at[off, mine0],
                g0_send.at[off, side],
                g0_recv.at[off, lane],
                seg,
                dest,
            )
        )
    for off, dest in act_targets():
        send(
            remote(
                racts0.at[0, mine0],
                racts0.at[off, mine0],
                a0_send.at[off],
                a0_recv.at[off, lane],
                seg,
                dest,
            )
        )
    for off in range(1, segs):
        pl.semaphore_signal(
            ready, inc=1, device_id=(lax.rem(seg + off, segs), blk), device_id_type=MESH
        )

    full = counts[blk] == SLOTS
    sel_a.wait_recv()
    picked = jnp.where(full, acts[keep, :].astype(F32), other_a[...].astype(F32)).astype(B16)
    racts1[0, mine1] = jnp.dot(picked, b_in[...], preferred_element_type=F32).astype(B16)
    for off, dest in act_targets():
        send(
            remote(
                racts1.at[0, mine1],
                racts1.at[off, mine1],
                a1_send.at[off],
                a1_recv.at[off, lane],
                seg,
                dest,
            )
        )

    l_own.wait()
    sel_g.wait_recv()
    own_g[...] = jnp.where(full, own_g[...].astype(F32), other_g[...].astype(F32)).astype(B16)
    for off, side, dest in targets():
        send(
            remote(
                own_g.at[:, cols(dest)],
                grads1.at[off, mine1],
                g1_send.at[off, side],
                g1_recv.at[off, lane],
                seg,
                dest,
            )
        )
    own1 = pltpu.make_async_copy(own_g.at[:, cols(blk)], grads1.at[0, mine1], g1_recv.at[0, lane])
    own1.start()

    l_qacts.wait()
    rot_q[...] = jnp.dot(qacts[...], b_in[...], preferred_element_type=F32).astype(B16)
    l_eig.wait()
    inv[...] = 1.0 / (eig[...].astype(F32) + damping)
    l_bout.wait()

    @pl.when(jnp.logical_and(seg > 0, seg < segs - 1))
    def _():
        for q in range(queries):
            e_copy(q).wait_recv()
            advance(q)
            e_copy(q).start()

    def arrived(buf, sem, i, side, size):
        ref = buf.at[i, pl.ds(pl.multiple_of(side * size, size), size)]
        remote(ref, ref, sel_send.at[0], sem.at[i, side], seg, mate).wait_recv()

    for buf, sem, fsem, rows_of, size in (
        (racts0, a0_recv, f0_send, mine0, tb),
        (racts1, a1_recv, f1_send, mine1, half),
    ):
        for off in range(1, chips):
            arrived(buf, sem, off, lane, size)
            ref = buf.at[off, rows_of]
            send(remote(ref, ref, fsem.at[off], sem.at[off, lane], seg, mate))

    for i in range(chips):
        for side in range(2):
            arrived(grads0, g0_recv, i, side, tb)
        turned0[i] = jnp.dot(grads0[i], b_out[...], preferred_element_type=F32).astype(B16)
    for i in range(chips):
        arrived(racts0, a0_recv, i, mate_lane, tb)

    def core_of(q):
        return core_all[:, q * width : (q + 1) * width]

    def folded(x):
        x = sum(x[:, n * 128 : (n + 1) * 128] for n in range(width // 128))
        return jnp.sum(x, axis=0, keepdims=True)

    for q in range(queries):

        @pl.when(seg == 0)
        def _():
            e_copy(q).wait_recv()

        r = pl.ds(q * qt, qt)
        rot_e = jnp.dot(errs[r], b_out[...], preferred_element_type=F32).astype(B16)
        raw = lax.dot_general(
            rot_e, rot_q[r], (((0,), (0,)), ((), ())), preferred_element_type=F32
        )
        core_all[:, q * width : (q + 1) * width] = (raw * inv[...]).astype(B16)
        for i in range(chips):
            h = jnp.dot(turned0[i], core_of(q), preferred_element_type=F32)
            prod = h * racts0[i].astype(F32)
            for side in range(2):
                part[i, side, q : q + 1, :] = folded(prod[side * tb : (side + 1) * tb])

    for i in range(chips):
        for side in range(2):
            arrived(grads1, g1_recv, i, side, half)
        arrived(racts1, a1_recv, i, mate_lane, half)
    late = jnp.dot(
        grads1[...].reshape(chips * tb, width), b_out[...], preferred_element_type=F32
    ).astype(B16)
    for q in range(queries):
        h = jnp.dot(late, core_of(q), preferred_element_type=F32)
        prod = h * racts1[...].reshape(chips * tb, width).astype(F32)
        for i in range(chips):
            shared = folded(prod[i * tb : (i + 1) * tb])
            for side in range(2):
                part[i, side, queries + q : queries + q + 1, :] = shared

    values = 2 * queries
    tile = (chips, 2, values, 128)
    diag = lax.broadcasted_iota(jnp.int32, tile, 2) == lax.broadcasted_iota(jnp.int32, tile, 3)
    sums = jnp.sum(part[...], axis=3, keepdims=True)
    packed[...] = jnp.sum(jnp.where(diag, sums, 0.0), axis=2, keepdims=True)

    pl.semaphore_wait(ready, segs - 1)
    for seg_off in range(segs - 1, -1, -1):
        seg_to = lax.rem(seg + seg_off, segs)
        for off in range(chips):
            chip_to = lax.rem(chip + chips - off, chips)
            for turn in range(2):
                if seg_off == 0 and off == 0 and turn == 0:
                    continue
                side = lane if turn == 0 else mate_lane
                send(
                    remote(
                        packed.at[off, side],
                        gathered.at[seg, blk],
                        p_send.at[seg_off, off, turn],
                        p_recv.at[seg, blk],
                        seg_to,
                        chip_to * 2 + side,
                    )
                )
    gathered[seg, blk] = packed[0, lane]
    for seg_off in range(segs):
        for off in range(blks):
            if seg_off == 0 and off == 0:
                continue
            a, b = lax.rem(seg + seg_off, segs), lax.rem(blk + off, blks)
            ref = gathered.at[a, b]
            remote(ref, ref, sel_send.at[0], p_recv.at[a, b], seg, mate).wait_recv()
    total = jnp.sum(gathered[...].reshape(segs * blks, 128), axis=0, keepdims=True)
    tile = (values, 128)
    diag = lax.broadcasted_iota(jnp.int32, tile, 0) == lax.broadcasted_iota(jnp.int32, tile, 1)
    total = jnp.sum(jnp.where(diag, jnp.broadcast_to(total, tile), 0.0), axis=1, keepdims=True)
    out[:, 0:1] = total[0:queries]
    out[:, 1:2] = total[queries:values] * jnp.where(full, 1.0, 0.0)

    for copy in sends:
        copy.wait_send()

    @pl.when(seg > 0)
    def _():
        for q in range(queries):
            e_copy(q).wait_send()


def body(
    train_acts,
    train_grads,
    counts,
    basis_in,
    basis_out,
    eigenvalues,
    back_weight,
    derivative,
    query_acts,
    query_top,
):
    segs = lax.axis_size("seg")
    blks = lax.axis_size("blk")
    chips = blks // 2
    queries, qt, width = query_top.shape
    rows = train_acts.shape[1]
    tb = rows // SLOTS
    half = tb // 2
    wide = train_grads.shape[2]
    any_spec = pl.BlockSpec(memory_space=pltpu.HBM)
    vm = pltpu.VMEM
    dma = pltpu.SemaphoreType.DMA
    return pl.pallas_call(
        functools.partial(kernel, segs, blks, queries),
        out_shape=jax.ShapeDtypeStruct((queries, SLOTS), F32),
        in_specs=[pl.BlockSpec(memory_space=pltpu.SMEM)] + [any_spec] * 9,
        out_specs=pl.BlockSpec(memory_space=pltpu.VMEM),
        scratch_shapes=[
            vm((rows, width), B16),
            vm((half, wide), B16),
            vm((half, wide), B16),
            vm((half, width), B16),
            vm((width, width), B16),
            vm((width, width), B16),
            vm((width, width), B16),
            vm((width, width), B16),
            vm((queries * qt, width), B16),
            vm((queries * qt, width), B16),
            vm((queries * qt, width), B16),
            vm((queries * qt, width), B16),
            vm((width, width), F32),
            vm((queries * qt, width), B16),
            vm((width, queries * width), B16),
            vm((chips, 2 * tb, width), B16),
            vm((chips, 2 * half, width), B16),
            vm((chips, 2 * tb, width), B16),
            vm((chips, 2 * half, width), B16),
            vm((chips, 2 * tb, width), B16),
            vm((chips, 2, 2 * queries, 128), F32),
            vm((chips, 2, 1, 128), F32),
            vm((segs, blks, 1, 128), F32),
            dma((9,)),
            dma((2,)),
            dma((2,)),
            dma((chips, 2)),
            dma((chips, 2)),
            dma((chips, 2)),
            dma((chips, 2)),
            dma((chips,)),
            dma((chips, 2)),
            dma((chips,)),
            dma((chips, 2)),
            dma((chips,)),
            dma((chips,)),
            dma((queries,)),
            dma((queries,)),
            dma((segs, chips, 2)),
            dma((segs, blks)),
            pltpu.SemaphoreType.REGULAR,
        ],
        compiler_params=pltpu.CompilerParams(
            collective_id=0, has_side_effects=True, vmem_limit_bytes=67_043_328
        ),
    )(
        counts,
        train_acts[0],
        train_grads[0],
        basis_in[0, 0],
        basis_out[0, 0],
        eigenvalues[0, 0],
        back_weight[0, 0],
        derivative[0].reshape(queries * qt, width),
        query_acts[0].reshape(queries * qt, width),
        query_top.reshape(queries * qt, width),
    )


def solution(mesh):
    in_specs = (
        P("seg", "blk", None),
        P("seg", "blk", None),
        P(),
        P("seg", None, None, None),
        P("seg", "blk", None, None),
        P("seg", "blk", None, None),
        P("seg", "blk", None, None),
        P("seg", None, None, "blk"),
        P("seg", None, None, None),
        P(None, None, "blk"),
    )
    out_specs = P(None, "blk")
    return jax.shard_map(body, mesh=mesh, in_specs=in_specs, out_specs=out_specs, check_vma=False)
```

time: 33.3 us -> 33.2 us (level)
  no operation moved by 1% of the time
where the time goes in v3:
time: 33.2 us; the launch traced here: 33 us
  Pallas kernels  31.7 us (95%)
  local copies, waits for them, and re-layouts  1.32 us (4%)
    pallas_call x1, Pallas kernels, body(): pl.pallas_call(functools.partial(kernel, segs, blks, queries), out_shape=...  31.7 us
    pallas_call x1, local copies, waits for them, and re-layouts, body(): pl.pallas_call(functools.partial(kernel, segs, blks, queries), out_shape=...  1.32 us

profile of v3, /device:TPU:0, one launch (start us, length us, event | category | flops | bytes accessed | tf_op | source)
XLA Modules:
  0.0 33.0 jit_solution(8839560427025492082)
XLA Ops:
  0.0 31.7 %shard_map.100 = f32[4,2]{1,0:T(4,128)} custom-call(s32[8]{0:T(128)} %counts.1, bf16[128,512]{1,0:T(8,128)(2,1)} %bitcast.14, bf16[128,4096]{1,0:T(8,128)(2,1)} %bitcast.9, bf16[512,512]{1,0:T(8,128)(2,1)} %bitcast.10, bf16[512,512]{1,0:T(8,128)(2,1)} %bitcast.11, bf16[512,512]{1,0:T(8,128)(2,1)} %bitcast.12, bf16[512,512]{1,0:T(8,128)(2,1)} %bitcast.13, ...), custom_call_target="tpu_custom_call" | custom-call | tf_op jit(solution)/shard_map/pallas_call | solution.py:410
  31.7 1.3 %copy.11 = f32[4,2]{0,1:T(2,128)} copy(f32[4,2]{1,0:T(4,128)} %shard_map.100) | data formatting | bytes 64 | tf_op jit(solution)/shard_map/pallas_call | solution.py:410

commit v4 on v3

--- a/solution.py
+++ b/solution.py
@@ -167,10 +167,6 @@
         for q in range(queries):
             advance(q)
 
-    l_acts.wait()
-    l_bin.wait()
-    racts0[0, mine0] = jnp.dot(acts[0:tb], b_in[...], preferred_element_type=F32).astype(B16)
-
     pl.semaphore_wait(barrier, blks - 1 + segs - 1)
 
     @pl.when(seg == segs - 1)
@@ -213,6 +209,10 @@
                 dest,
             )
         )
+    l_acts.wait()
+    l_bin.wait()
+    racts0[0, mine0] = jnp.dot(acts[0:tb], b_in[...], preferred_element_type=F32).astype(B16)
+
     for off, dest in act_targets():
         send(
             remote(
@@ -279,19 +279,18 @@
         ref = buf.at[i, pl.ds(pl.multiple_of(side * size, size), size)]
         remote(ref, ref, sel_send.at[0], sem.at[i, side], seg, mate).wait_recv()
 
-    for buf, sem, fsem, rows_of, size in (
-        (racts0, a0_recv, f0_send, mine0, tb),
-        (racts1, a1_recv, f1_send, mine1, half),
-    ):
+    def forward(buf, sem, fsem, rows_of, size):
         for off in range(1, chips):
             arrived(buf, sem, off, lane, size)
             ref = buf.at[off, rows_of]
             send(remote(ref, ref, fsem.at[off], sem.at[off, lane], seg, mate))
 
+    forward(racts0, a0_recv, f0_send, mine0, tb)
     for i in range(chips):
         for side in range(2):
             arrived(grads0, g0_recv, i, side, tb)
         turned0[i] = jnp.dot(grads0[i], b_out[...], preferred_element_type=F32).astype(B16)
+    forward(racts1, a1_recv, f1_send, mine1, half)
     for i in range(chips):
         arrived(racts0, a0_recv, i, mate_lane, tb)
 

time: 33.2 us -> 32.2 us (0.970)
  Pallas kernels: 31.7 us -> 30.7 us
    pallas_call x1, Pallas kernels: 31.7 us -> 30.7 us  [body(): pl.pallas_call(functools.partial(kernel, segs, blks, queries), out_shape=...]
where the time goes in v4:
time: 32.2 us; the launch traced here: 32.1 us
  Pallas kernels  30.7 us (95%)
  local copies, waits for them, and re-layouts  1.32 us (4%)
    pallas_call x1, Pallas kernels, body(): pl.pallas_call(functools.partial(kernel, segs, blks, queries), out_shape=...  30.7 us
    pallas_call x1, local copies, waits for them, and re-layouts, body(): pl.pallas_call(functools.partial(kernel, segs, blks, queries), out_shape=...  1.32 us

profile of v4, /device:TPU:0, one launch (start us, length us, event | category | flops | bytes accessed | tf_op | source)
XLA Modules:
  0.0 32.1 jit_solution(9520679499389063699)
XLA Ops:
  0.0 30.7 %shard_map.100 = f32[4,2]{1,0:T(4,128)} custom-call(s32[8]{0:T(128)} %counts.1, bf16[128,512]{1,0:T(8,128)(2,1)} %bitcast.14, bf16[128,4096]{1,0:T(8,128)(2,1)} %bitcast.9, bf16[512,512]{1,0:T(8,128)(2,1)} %bitcast.10, bf16[512,512]{1,0:T(8,128)(2,1)} %bitcast.11, bf16[512,512]{1,0:T(8,128)(2,1)} %bitcast.12, bf16[512,512]{1,0:T(8,128)(2,1)} %bitcast.13, ...), custom_call_target="tpu_custom_call" | custom-call | tf_op jit(solution)/shard_map/pallas_call | solution.py:409
  30.8 1.3 %copy.11 = f32[4,2]{0,1:T(2,128)} copy(f32[4,2]{1,0:T(4,128)} %shard_map.100) | data formatting | bytes 64 | tf_op jit(solution)/shard_map/pallas_call | solution.py:409
